TPU v7x, 512 devices: a whole 4x8x8 slice. The times are simulated.
512 devices in a mesh: ctx: 64 (over z_hi, y, core), tp: 8 (over x, z_lo).
Axes of the slice: x: 4, y: 8, z: 8 (z_hi: 4, z_lo: 2; z = z_hi * 2 + z_lo), core: 2. Of those that a mesh axis runs over, the one named last changes fastest.
Arguments:
- query_in: bfloat16 [1024, 16384], P('tp', 'ctx'), may hold values from -6 to 6
- key_in: bfloat16 [1024, 16384], P('tp', 'ctx'), may hold values from -6 to 6
- value_in: bfloat16 [1024, 16384], P('tp', 'ctx'), may hold values from -6 to 6
- short_kernel: float32 [3, 1024, 7], P(None, 'tp'), may hold values from -2 to 2
- basis_weight: float32 [64, 33], replicated, may hold values from -96 to 96
- basis_bias: float32 [64], replicated, may hold values from -3.140625 to 3.140625
- filter_proj: float32 [1024, 64], P('tp'), may hold values from -0.75 to 0.75
- decay_rate: float32 [1024], P('tp'), as said below
- skip_gain: float32 [1024], P('tp'), may hold values from -3 to 3
- grad_out: bfloat16 [1024, 16384], P('tp', 'ctx'), may hold values from -6 to 6
Outputs:
- mixed: bfloat16 [1024, 16384], P('tp', 'ctx')
- grad_query: bfloat16 [1024, 16384], P('tp', 'ctx')
- grad_key: bfloat16 [1024, 16384], P('tp', 'ctx')
- grad_value: bfloat16 [1024, 16384], P('tp', 'ctx')
- grad_proj: float32 [1024, 64], P('tp')
- grad_basis: float32 [64, 33], replicated
Inputs may be any that keep to these rules, and one draw needn't show every extreme that they name: decay_rate is positive in every channel.
All inputs are finite; a program needn't handle non-finite values.
Results may differ from a plain program's by a relative error of at most 0.0066.
Values may be sent and summed in bfloat16 or wider, within the bound.
No kernel may reach another device: no remote copies, remote signals or barrier semaphores. Data moves between devices by JAX's collectives and lax.ppermute only.
A program may use at most 64 MiB of HBM per device.

v0:
```python
import math
import jax
import jax.numpy as jnp
from jax import lax
from jax.sharding import PartitionSpec as P

PRECISE = lax.Precision.HIGHEST


def passed_along(value, axis, steps):
    count = lax.axis_size(axis)
    leading, last = (max(0, -steps), min(count, count - steps))
    return lax.ppermute(value, axis, [(source, source + steps) for source in range(leading, last)])


def features(offset_pos, num_pos, seq_total, num_freq):
    positions = offset_pos + jnp.arange(num_pos, dtype=jnp.int32)
    pieces = [positions.astype(jnp.float32) / seq_total]
    for harmonic in range(1, num_freq + 1):
        angles = (harmonic * positions % seq_total).astype(jnp.float32) * (
            2.0 * math.pi / seq_total
        )
        pieces.append(jnp.cos(angles))
        pieces.append(jnp.sin(angles))
    return jnp.stack(pieces)


def window(decay_rate, offset_pos, num_pos, seq_total):
    positions = (offset_pos + jnp.arange(num_pos, dtype=jnp.int32)).astype(jnp.float32)
    energy = jnp.expm1(-2.0 * decay_rate) / jnp.expm1(-2.0 * decay_rate / seq_total)
    return (
        jnp.exp(-(decay_rate[:, None] * positions[None, :]) / seq_total) / jnp.sqrt(energy)[:, None]
    )


def featurize_rim(signal, before, kernel):
    extended = jnp.concatenate([before, signal], axis=1).astype(jnp.float32)
    num_taps = kernel.shape[1]
    rim_len = num_taps - 1
    num_tok = signal.shape[1]
    result = kernel[:, 0:1] * extended[:, rim_len:]
    for offset in range(1, num_taps):
        result = (
            result
            + kernel[:, offset : offset + 1]
            * extended[:, rim_len - offset : rim_len - offset + num_tok]
        )
    return result


def featurize_back(signal, following, kernel):
    extended = jnp.concatenate([signal, following], axis=1).astype(jnp.float32)
    num_taps = kernel.shape[1]
    num_tok = signal.shape[1]
    result = kernel[:, 0:1] * extended[:, :num_tok]
    for offset in range(1, num_taps):
        result = result + kernel[:, offset : offset + 1] * extended[:, offset : offset + num_tok]
    return result


def tables(num_rows, num_cols, modulus):
    row_ids = jnp.arange(num_rows, dtype=jnp.int32)[:, None]
    col_ids = jnp.arange(num_cols, dtype=jnp.int32)[None, :]
    angles = (row_ids * col_ids % modulus).astype(jnp.float32) * (-2.0 * math.pi / modulus)
    return (jnp.cos(angles), jnp.sin(angles))


def spectrum(signal, outer, twiddle, inner):
    num_chan = signal.shape[0]
    folded = signal.reshape(num_chan, outer[0].shape[1], inner[0].shape[0])
    section_re = jnp.einsum("kt,nts->nks", outer[0], folded, precision=PRECISE)
    section_im = jnp.einsum("kt,nts->nks", outer[1], folded, precision=PRECISE)
    turned_re = section_re * twiddle[0] - section_im * twiddle[1]
    turned_im = section_re * twiddle[1] + section_im * twiddle[0]
    spec_re = jnp.einsum("nks,sj->nkj", turned_re, inner[0], precision=PRECISE) - jnp.einsum(
        "nks,sj->nkj", turned_im, inner[1], precision=PRECISE
    )
    spec_im = jnp.einsum("nks,sj->nkj", turned_re, inner[1], precision=PRECISE) + jnp.einsum(
        "nks,sj->nkj", turned_im, inner[0], precision=PRECISE
    )
    return (spec_re, spec_im)


def restore(spec_re, spec_im, outer, twiddle, inner):
    num_chan = spec_re.shape[0]
    padded_len = outer[0].shape[0] * inner[0].shape[0]
    back_re = jnp.einsum("nkj,sj->nks", spec_re, inner[0], precision=PRECISE) + jnp.einsum(
        "nkj,sj->nks", spec_im, inner[1], precision=PRECISE
    )
    back_im = jnp.einsum("nkj,sj->nks", spec_im, inner[0], precision=PRECISE) - jnp.einsum(
        "nkj,sj->nks", spec_re, inner[1], precision=PRECISE
    )
    turned_re = back_re * twiddle[0] + back_im * twiddle[1]
    turned_im = back_im * twiddle[0] - back_re * twiddle[1]
    result = jnp.einsum("kt,nks->nts", outer[0], turned_re, precision=PRECISE) + jnp.einsum(
        "kt,nks->nts", outer[1], turned_im, precision=PRECISE
    )
    return result.reshape(num_chan, -1) * (1.0 / padded_len)


def convolve_forward(carried_chan, filter_chan, own_skip, transform_tables):
    outer, twiddle, inner = transform_tables
    carried_wide = carried_chan.astype(jnp.float32)
    carried_re, carried_im = spectrum(carried_wide, outer, twiddle, inner)
    filter_re, filter_im = spectrum(filter_chan.astype(jnp.float32), outer, twiddle, inner)
    conv_chan = restore(
        filter_re * carried_re - filter_im * carried_im,
        filter_re * carried_im + filter_im * carried_re,
        outer,
        twiddle,
        inner,
    )
    long_chan = (conv_chan + own_skip[:, None] * carried_wide).astype(jnp.bfloat16)
    return (long_chan, (carried_re, carried_im, filter_re, filter_im))


def convolve_backward(grad_chan, spectra, own_skip, transform_tables):
    outer, twiddle, inner = transform_tables
    carried_re, carried_im, filter_re, filter_im = spectra
    grad_chan_wide = grad_chan.astype(jnp.float32)
    grad_re, grad_im = spectrum(grad_chan_wide, outer, twiddle, inner)
    carried_grad_chan = (
        restore(
            filter_re * grad_re + filter_im * grad_im,
            filter_re * grad_im - filter_im * grad_re,
            outer,
            twiddle,
            inner,
        )
        + own_skip[:, None] * grad_chan_wide
    ).astype(jnp.bfloat16)
    filter_grad_chan = restore(
        carried_re * grad_re + carried_im * grad_im,
        carried_re * grad_im - carried_im * grad_re,
        outer,
        twiddle,
        inner,
    ).astype(jnp.bfloat16)
    return (carried_grad_chan, filter_grad_chan)


def on_device(
    query_in,
    key_in,
    value_in,
    short_kernel,
    basis_weight,
    basis_bias,
    filter_proj,
    decay_rate,
    skip_gain,
    grad_out,
):
    ctx_size = lax.axis_size("ctx")
    ctx_rank = lax.axis_index("ctx")
    tp_size = lax.axis_size("tp")
    num_tok = query_in.shape[1]
    chan_local = query_in.shape[0]
    seq_total = num_tok * ctx_size
    all_channels = chan_local * tp_size
    num_freq = (basis_weight.shape[1] - 1) // 2
    feat_width = basis_weight.shape[0]
    rim_len = short_kernel.shape[2] - 1
    tok_start = ctx_rank * num_tok
    rim_edge = num_tok - rim_len
    per_dev = chan_local // ctx_size
    chan_start = ctx_rank * per_dev
    own_skip = lax.dynamic_slice_in_dim(skip_gain, chan_start, per_dev)
    proj_scale = 1.0 / math.sqrt(seq_total)
    basis_scale = math.sqrt(feat_width / (seq_total * all_channels))
    before = passed_along(
        (query_in[:, rim_edge:], key_in[:, rim_edge:], value_in[:, rim_edge:]), "ctx", 1
    )
    query_feat = featurize_rim(query_in, before[0], short_kernel[0])
    key_feat = featurize_rim(key_in, before[1], short_kernel[1])
    value_feat = featurize_rim(value_in, before[2], short_kernel[2])
    carried = (key_feat * value_feat).astype(jnp.bfloat16)
    grad_wide = grad_out.astype(jnp.float32)
    grad_long = (grad_wide * query_feat).astype(jnp.bfloat16)
    basis_rows = features(tok_start, num_tok, seq_total, num_freq)
    hidden_in = (
        jnp.dot(basis_weight, basis_rows, precision=PRECISE, preferred_element_type=jnp.float32)
        + basis_bias[:, None]
    )
    activation = jnp.sin(hidden_in)
    envelope = window(decay_rate, tok_start, num_tok, seq_total)
    filter_tok = (
        jnp.dot(filter_proj, activation, precision=PRECISE, preferred_element_type=jnp.float32)
        * envelope
    ).astype(jnp.bfloat16)
    inner_len = 2 * ctx_size
    transform_tables = (
        tables(num_tok, num_tok // 2, num_tok),
        tables(num_tok, inner_len, 2 * seq_total),
        tables(inner_len, inner_len, inner_len),
    )
    spread = (
        lax.all_to_all(carried, "ctx", split_axis=0, concat_axis=1, tiled=True),
        lax.all_to_all(filter_tok, "ctx", split_axis=0, concat_axis=1, tiled=True),
    )
    carried_chan = spread[0]
    filter_chan = spread[1]
    long_chan, spectra = convolve_forward(carried_chan, filter_chan, own_skip, transform_tables)
    long_tok = lax.all_to_all(long_chan, "ctx", split_axis=1, concat_axis=0, tiled=True)
    grad_chan = lax.all_to_all(grad_long, "ctx", split_axis=0, concat_axis=1, tiled=True)
    carried_grad_chan, filter_grad_chan = convolve_backward(
        grad_chan, spectra, own_skip, transform_tables
    )
    returned = (
        lax.all_to_all(carried_grad_chan, "ctx", split_axis=1, concat_axis=0, tiled=True),
        lax.all_to_all(filter_grad_chan, "ctx", split_axis=1, concat_axis=0, tiled=True),
    )
    carried_grad = returned[0]
    filter_grad_tok = returned[1]
    long_wide = long_tok.astype(jnp.float32)
    mixed = (query_feat * long_wide).astype(jnp.bfloat16)
    grad_query_feat = (grad_wide * long_wide).astype(jnp.bfloat16)
    grad_raw = filter_grad_tok.astype(jnp.float32) * envelope
    part_proj = jnp.dot(
        grad_raw, activation.T, precision=PRECISE, preferred_element_type=jnp.float32
    )
    grad_hidden = jnp.dot(
        filter_proj.T, grad_raw, precision=PRECISE, preferred_element_type=jnp.float32
    ) * jnp.cos(hidden_in)
    part_basis = jnp.dot(
        grad_hidden, basis_rows.T, precision=PRECISE, preferred_element_type=jnp.float32
    )
    grad_proj = lax.psum(part_proj, "ctx") * proj_scale
    grad_basis = lax.psum(part_basis, ("ctx", "tp")) * basis_scale
    carried_grad_wide = carried_grad.astype(jnp.float32)
    grad_key_feat = (carried_grad_wide * value_feat).astype(jnp.bfloat16)
    grad_value_feat = (carried_grad_wide * key_feat).astype(jnp.bfloat16)
    following = passed_along(
        (grad_query_feat[:, :rim_len], grad_key_feat[:, :rim_len], grad_value_feat[:, :rim_len]),
        "ctx",
        -1,
    )
    grad_query = featurize_back(grad_query_feat, following[0], short_kernel[0]).astype(jnp.bfloat16)
    grad_key = featurize_back(grad_key_feat, following[1], short_kernel[1]).astype(jnp.bfloat16)
    grad_value = featurize_back(grad_value_feat, following[2], short_kernel[2]).astype(jnp.bfloat16)
    return (mixed, grad_query, grad_key, grad_value, grad_proj, grad_basis)


def solution(mesh):
    return jax.shard_map(
        on_device,
        mesh=mesh,
        in_specs=(
            P("tp", "ctx"),
            P("tp", "ctx"),
            P("tp", "ctx"),
            P(None, "tp", None),
            P(),
            P(),
            P("tp", None),
            P("tp"),
            P("tp"),
            P("tp", "ctx"),
        ),
        out_specs=(
            P("tp", "ctx"),
            P("tp", "ctx"),
            P("tp", "ctx"),
            P("tp", "ctx"),
            P("tp", None),
            P(),
        ),
        check_vma=False,
    )
```

profile of v0, /device:TPU:1, one launch (start us, length us, event | category | flops | bytes accessed | tf_op | source)
XLA Modules:
  0.0 538.5 jit_solution(8369667688324918726)
XLA Ops:
  0.6 0.8 slice.242
  1.5 4.6 collective-permute-start
  10.4 15.5 %all-to-all-start = ((bf16[64,2,256]{2,1,0:T(2,128)(2,1)}), bf16[64,2,256]{2,1,0:T(2,128)(2,1)S(1)}, u32[]{:S(2)}, u32[]{:S(2)}) async-start(bf16[64,2,256]{2,1,0:T(2,128)(2,1)} %all_to_all.60), calls=%async_computation | async-start | bytes 131072 | tf_op jit(solution)/shard_map/all_to_all | solution.py:199
  26.0 3.5 collective-permute-start.2
  29.6 2.2 collective-permute-start.1
  35.7 2.4 all-to-all-done
  38.1 9.7 %all-to-all-start.3 = ((bf16[64,2,256]{2,1,0:T(2,128)(2,1)}), bf16[64,2,256]{2,1,0:T(2,128)(2,1)S(1)}, u32[]{:S(2)}, u32[]{:S(2)}) async-start(bf16[64,2,256]{2,1,0:T(2,128)(2,1)} %all_to_all.67), calls=%async_computation.3 | async-start | bytes 131072 | tf_op jit(solution)/shard_map/all_to_all | solution.py:205
  51.7 7.9 %all-to-all-done.3 = bf16[64,2,256]{2,1,0:T(2,128)(2,1)S(1)} async-done(((bf16[64,2,256]{2,1,0:T(2,128)(2,1)}), bf16[64,2,256]{2,1,0:T(2,128)(2,1)S(1)}, u32[]{:S(2)}, u32[]{:S(2)}) %all-to-all-start.3) | async-done | bytes 65568 | tf_op jit(solution)/shard_map/all_to_all | solution.py:205
  60.4 0.8 convolution_bitcast_fusion.1
  67.6 11.5 %fusion.19 = f32[2,128,128]{2,1,0:T(8,128)S(1)} fusion(f32[2,256,128]{1,2,0:T(8,128)S(1)} %convolution_subtract_fusion.1, f32[2,256,128]{1,2,0:T(8,128)S(1)} %convolution_add_fusion.1, f32[256,128]{0,1:T(8,128)S(1)} %copy.206, f32[256,128]{0,1:T(8,128)S(1)} %copy.204), kind=kOutput, calls=%fused_computation.45 | convolution fusion | flops 101318656 | bytes 917504 | tf_op jit(solution)/shard_map/kt,nks->nts/dot_general | solution.py:95
  79.1 0.9 fusion.2
  80.9 4.8 all-to-all-start.4
  86.0 12.0 %all-to-all-done.4 = bf16[2,64,256]{2,0,1:T(2,128)(2,1)S(1)} async-done(((bf16[2,64,256]{2,0,1:T(2,128)(2,1)}), bf16[2,64,256]{2,0,1:T(2,128)(2,1)S(1)}, u32[]{:S(2)}, u32[]{:S(2)}) %all-to-all-start.4) | async-done | bytes 65568 | tf_op jit(solution)/shard_map/all_to_all | solution.py:210
  98.5 2.3 collective-permute-start.5
  101.9 6.0 %all-to-all-start.1 = ((bf16[64,2,256]{2,1,0:T(2,128)(2,1)}), bf16[64,2,256]{2,1,0:T(2,128)(2,1)S(1)}, u32[]{:S(2)}, u32[]{:S(2)}) async-start(bf16[64,2,256]{2,1,0:T(2,128)(2,1)} %all_to_all.63), calls=%async_computation.1 | async-start | bytes 131072 | tf_op jit(solution)/shard_map/all_to_all | solution.py:198
  108.0 2.4 collective-permute-start.4
  110.4 1.0 fusion.37
  111.4 2.1 collective-permute-done.4
  113.5 1.0 fusion.44
  114.5 5.6 %all-to-all-done.1 = bf16[64,2,256]{2,1,0:T(2,128)(2,1)S(1)} async-done(((bf16[64,2,256]{2,1,0:T(2,128)(2,1)}), bf16[64,2,256]{2,1,0:T(2,128)(2,1)S(1)}, u32[]{:S(2)}, u32[]{:S(2)}) %all-to-all-start.1) | async-done | bytes 65568 | tf_op jit(solution)/shard_map/all_to_all | solution.py:198
  124.0 0.8 multiply_add_fusion
  127.4 0.9 fusion.12
  128.3 0.9 fusion.8
  130.0 7.0 %all-to-all-start.5 = ((bf16[2,64,256]{2,0,1:T(2,128)(2,1)}), bf16[2,64,256]{2,0,1:T(2,128)(2,1)S(1)}, u32[]{:S(2)}, u32[]{:S(2)}) async-start(bf16[2,64,256]{2,0,1:T(2,128)(2,1)} %copy.242), calls=%async_computation.5 | async-start | bytes 131072 | tf_op jit(solution)/shard_map/all_to_all | solution.py:211
  139.6 0.9 fusion.26
  140.5 0.9 fusion.4
  142.3 6.9 %all-to-all-done.5 = bf16[2,64,256]{2,0,1:T(2,128)(2,1)S(1)} async-done(((bf16[2,64,256]{2,0,1:T(2,128)(2,1)}), bf16[2,64,256]{2,0,1:T(2,128)(2,1)S(1)}, u32[]{:S(2)}, u32[]{:S(2)}) %all-to-all-start.5) | async-done | bytes 65568 | tf_op jit(solution)/shard_map/all_to_all | solution.py:211
  149.2 5.8 %all-to-all-start.2 = ((bf16[2,64,256]{2,0,1:T(2,128)(2,1)}), bf16[2,64,256]{2,0,1:T(2,128)(2,1)S(1)}, u32[]{:S(2)}, u32[]{:S(2)}) async-start(bf16[2,64,256]{2,0,1:T(2,128)(2,1)} %copy.223), calls=%async_computation.2 | async-start | bytes 131072 | tf_op jit(solution)/shard_map/all_to_all | solution.py:204
  156.2 99.6 %psum.15 = f32[64,33]{0,1:T(8,128)S(1)} all-reduce(f32[64,33]{0,1:T(8,128)S(1)} %fusion.423), channel_id=1, replica_groups=mesh['ctx'=64,'tp'=8] {'ctx','tp'}, use_global_device_ids=true, to_apply=%region_1.2 | all-reduce | flops 2112 | bytes 16896 | tf_op jit(solution)/shard_map/psum | solution.py:229
  255.8 270.7 %psum.14 = f32[128,64]{0,1:T(8,128)S(1)} all-reduce(f32[128,64]{0,1:T(8,128)S(1)} %fusion.417), channel_id=1, replica_groups=mesh['ctx'=64,'tp'=8] {'ctx'}, use_global_device_ids=true, to_apply=%region_0.1 | all-reduce | flops 8192 | bytes 65536 | tf_op jit(solution)/shard_map/psum | solution.py:228
  528.0 8.4 %collective-permute-start.3 = (bf16[128,6]{1,0:T(8,128)(2,1)S(1)}, bf16[128,6]{1,0:T(8,128)(2,1)S(1)}, u32[]{:S(2)}, u32[]{:S(2)}) collective-permute-start(bf16[128,6]{1,0:T(8,128)(2,1)S(1)} %slice.333), channel_id=1, source_target_pairs={{8,0},{16,8},{24,16},{32,24},{40,32},{48,40},{56,48},{64,56},{72,6... | collective-permute-start | bytes 4616 | tf_op jit(solution)/shard_map/ppermute | solution.py:13
  537.3 1.0 fusion.51
  (132 shorter events, 36.1 us)
Async XLA Ops:
  0.6 8.8 %copy-start = (f32[128,64]{0,1:T(8,128)S(1)}, f32[128,64]{0,1:T(8,128)}, u32[]{:S(2)}) copy-start(f32[128,64]{0,1:T(8,128)} %param.16) | copy-start | bytes 98308
  1.5 32.3 %collective-permute-start = (bf16[128,6]{1,0:T(8,128)(2,1)S(1)}, bf16[128,6]{1,0:T(8,128)(2,1)S(1)}, u32[]{:S(2)}, u32[]{:S(2)}) collective-permute-start(bf16[128,6]{1,0:T(8,128)(2,1)S(1)} %slice.242), channel_id=1, source_target_pairs={{0,8},{8,16},{16,24},{24,32},{32,40},{40,48},{48,56},{56,64},{64,7... | collective-permute-start | bytes 4616 | tf_op jit(solution)/shard_map/ppermute | solution.py:13
  7.5 0.7 copy-start.9
  8.2 0.7 copy-start.5
  8.2 0.7 copy-start.7
  10.4 15.5 %copy-start.3 = (bf16[128,256]{1,0:T(8,128)(2,1)S(1)}, bf16[128,256]{1,0:T(8,128)(2,1)}, u32[]{:S(2)}) copy-start(bf16[128,256]{1,0:T(8,128)(2,1)} %param.12) | copy-start | bytes 196612
  10.4 27.7 %all-to-all-start = ((bf16[64,2,256]{2,1,0:T(2,128)(2,1)}), bf16[64,2,256]{2,1,0:T(2,128)(2,1)S(1)}, u32[]{:S(2)}, u32[]{:S(2)}) async-start(bf16[64,2,256]{2,1,0:T(2,128)(2,1)} %all_to_all.60), calls=%async_computation | async-start | bytes 131072 | tf_op jit(solution)/shard_map/all_to_all | solution.py:199
  25.9 3.6 copy-start.4
  26.0 59.8 %collective-permute-start.2 = (bf16[128,6]{1,0:T(8,128)(2,1)S(1)}, bf16[128,6]{1,0:T(8,128)(2,1)S(1)}, u32[]{:S(2)}, u32[]{:S(2)}) collective-permute-start(bf16[128,6]{1,0:T(8,128)(2,1)S(1)} %slice.274), channel_id=1, source_target_pairs={{0,8},{8,16},{16,24},{24,32},{32,40},{40,48},{48,56},{56,64},{64,7... | collective-permute-start | bytes 4616 | tf_op jit(solution)/shard_map/ppermute | solution.py:13
  29.6 2.7 copy-start.6
  29.6 56.3 %collective-permute-start.1 = (bf16[128,6]{1,0:T(8,128)(2,1)S(1)}, bf16[128,6]{1,0:T(8,128)(2,1)S(1)}, u32[]{:S(2)}, u32[]{:S(2)}) collective-permute-start(bf16[128,6]{1,0:T(8,128)(2,1)S(1)} %slice.258), channel_id=1, source_target_pairs={{0,8},{8,16},{16,24},{24,32},{32,40},{40,48},{48,56},{56,64},{64,7... | collective-permute-start | bytes 4616 | tf_op jit(solution)/shard_map/ppermute | solution.py:13
  33.0 0.9 copy-start.2
  33.1 0.7 copy-start.8
  33.8 0.8 copy-start.1
  38.1 21.5 %all-to-all-start.3 = ((bf16[64,2,256]{2,1,0:T(2,128)(2,1)}), bf16[64,2,256]{2,1,0:T(2,128)(2,1)S(1)}, u32[]{:S(2)}, u32[]{:S(2)}) async-start(bf16[64,2,256]{2,1,0:T(2,128)(2,1)} %all_to_all.67), calls=%async_computation.3 | async-start | bytes 131072 | tf_op jit(solution)/shard_map/all_to_all | solution.py:205
  80.9 17.0 %all-to-all-start.4 = ((bf16[2,64,256]{2,0,1:T(2,128)(2,1)}), bf16[2,64,256]{2,0,1:T(2,128)(2,1)S(1)}, u32[]{:S(2)}, u32[]{:S(2)}) async-start(bf16[2,64,256]{2,0,1:T(2,128)(2,1)} %copy.236), calls=%async_computation.4 | async-start | bytes 131072 | tf_op jit(solution)/shard_map/all_to_all | solution.py:210
  98.5 11.8 %collective-permute-start.5 = (bf16[128,6]{1,0:T(8,128)(2,1)S(1)}, bf16[128,6]{1,0:T(8,128)(2,1)S(1)}, u32[]{:S(2)}, u32[]{:S(2)}) collective-permute-start(bf16[128,6]{1,0:T(8,128)(2,1)S(1)} %slice.349), channel_id=1, source_target_pairs={{8,0},{16,8},{24,16},{32,24},{40,32},{48,40},{56,48},{64,56},{72,6... | collective-permute-start | bytes 4616 | tf_op jit(solution)/shard_map/ppermute | solution.py:13
  101.9 18.2 %all-to-all-start.1 = ((bf16[64,2,256]{2,1,0:T(2,128)(2,1)}), bf16[64,2,256]{2,1,0:T(2,128)(2,1)S(1)}, u32[]{:S(2)}, u32[]{:S(2)}) async-start(bf16[64,2,256]{2,1,0:T(2,128)(2,1)} %all_to_all.63), calls=%async_computation.1 | async-start | bytes 131072 | tf_op jit(solution)/shard_map/all_to_all | solution.py:198
  108.0 5.5 %collective-permute-start.4 = (bf16[128,6]{1,0:T(8,128)(2,1)S(1)}, bf16[128,6]{1,0:T(8,128)(2,1)S(1)}, u32[]{:S(2)}, u32[]{:S(2)}) collective-permute-start(bf16[128,6]{1,0:T(8,128)(2,1)S(1)} %slice.341), channel_id=1, source_target_pairs={{8,0},{16,8},{24,16},{32,24},{40,32},{48,40},{56,48},{64,56},{72,6... | collective-permute-start | bytes 4616 | tf_op jit(solution)/shard_map/ppermute | solution.py:13
  130.0 19.1 %all-to-all-start.5 = ((bf16[2,64,256]{2,0,1:T(2,128)(2,1)}), bf16[2,64,256]{2,0,1:T(2,128)(2,1)S(1)}, u32[]{:S(2)}, u32[]{:S(2)}) async-start(bf16[2,64,256]{2,0,1:T(2,128)(2,1)} %copy.242), calls=%async_computation.5 | async-start | bytes 131072 | tf_op jit(solution)/shard_map/all_to_all | solution.py:211
  149.2 378.0 %all-to-all-start.2 = ((bf16[2,64,256]{2,0,1:T(2,128)(2,1)}), bf16[2,64,256]{2,0,1:T(2,128)(2,1)S(1)}, u32[]{:S(2)}, u32[]{:S(2)}) async-start(bf16[2,64,256]{2,0,1:T(2,128)(2,1)} %copy.223), calls=%async_computation.2 | async-start | bytes 131072 | tf_op jit(solution)/shard_map/all_to_all | solution.py:204
  528.0 9.3 %collective-permute-start.3 = (bf16[128,6]{1,0:T(8,128)(2,1)S(1)}, bf16[128,6]{1,0:T(8,128)(2,1)S(1)}, u32[]{:S(2)}, u32[]{:S(2)}) collective-permute-start(bf16[128,6]{1,0:T(8,128)(2,1)S(1)} %slice.333), channel_id=1, source_target_pairs={{8,0},{16,8},{24,16},{32,24},{40,32},{48,40},{56,48},{64,56},{72,6... | collective-permute-start | bytes 4616 | tf_op jit(solution)/shard_map/ppermute | solution.py:13
where the time goes:
time: 544 us; the launch traced here: 539 us
  blocking collectives  370 us (68%)
  starting transfers between devices  72.2 us (13%)
  matrix products  39.1 us (7%)
  waiting for transfers between devices  37.1 us (7%)
  other arithmetic  9.16 us (2%)
  local copies, waits for them, and re-layouts  8.96 us (2%)
    psum x1, blocking collectives, on_device(): grad_proj = lax.psum(part_proj, 'ctx') * proj_scale  271 us
    psum x1, blocking collectives, on_device(): grad_basis = lax.psum(part_basis, ('ctx', 'tp')) * basis_scale  99.6 us
    ppermute x6, starting transfers between devices, passed_along(): lax.ppermute(value, axis, [(source, source + steps) for source in range(l...  23.4 us
    all_to_all x1, starting transfers between devices, on_device(): lax.all_to_all(filter_tok, 'ctx', split_axis=0, concat_axis=1, tiled=True)  15.5 us
    dot_general x3, matrix products, restore(): jnp.einsum('kt,nks->nts', outer[0], turned_re, precision=PRECISE)  13.3 us
    all_to_all x1, waiting for transfers between devices, on_device(): lax.all_to_all(carried_grad_chan, 'ctx', split_axis=1, concat_axis=0, til...  12 us
  transfers between devices with their start and end apart: 12, of which 7 were waited for; matrix products, arithmetic and copies ran while one was open for 7% of the time, Pallas kernels for 0%

commit v1 on v0

--- a/solution.py
+++ b/solution.py
@@ -226,7 +226,7 @@
         grad_hidden, basis_rows.T, precision=PRECISE, preferred_element_type=jnp.float32
     )
     grad_proj = lax.psum(part_proj, "ctx") * proj_scale
-    grad_basis = lax.psum(part_basis, ("ctx", "tp")) * basis_scale
+    grad_basis = lax.psum(lax.psum(part_basis, axis_name="tp"), axis_name="ctx") * basis_scale
     carried_grad_wide = carried_grad.astype(jnp.float32)
     grad_key_feat = (carried_grad_wide * value_feat).astype(jnp.bfloat16)
     grad_value_feat = (carried_grad_wide * key_feat).astype(jnp.bfloat16)

time: 544 us -> 478 us (0.88)
  blocking collectives: 370 us -> 303 us
    psum x1, blocking collectives: 99.6 us -> 27.7 us  [on_device(): lax.psum(part_basis, axis_name='tp')]
  transfers between devices with their start and end apart: 12 -> 12, of which waited for: 7 -> 7; matrix products, arithmetic and copies ran while one was open for 7% -> 8% of each run, Pallas kernels for 0% -> 0%
where the time goes in v1:
time: 478 us; the launch traced here: 472 us
  blocking collectives  303 us (63%)
  starting transfers between devices  72.2 us (15%)
  matrix products  39.1 us (8%)
  waiting for transfers between devices  37.1 us (8%)
  other arithmetic  9.16 us (2%)
  local copies, waits for them, and re-layouts  8.96 us (2%)
    psum x1, blocking collectives, on_device(): grad_proj = lax.psum(part_proj, 'ctx') * proj_scale  276 us
    psum x1, blocking collectives, on_device(): lax.psum(part_basis, axis_name='tp')  27.7 us
    ppermute x6, starting transfers between devices, passed_along(): lax.ppermute(value, axis, [(source, source + steps) for source in range(l...  23.4 us
    all_to_all x1, starting transfers between devices, on_device(): lax.all_to_all(filter_tok, 'ctx', split_axis=0, concat_axis=1, tiled=True)  15.5 us
    dot_general x3, matrix products, restore(): jnp.einsum('kt,nks->nts', outer[0], turned_re, precision=PRECISE)  13.3 us
    all_to_all x1, waiting for transfers between devices, on_device(): lax.all_to_all(carried_grad_chan, 'ctx', split_axis=1, concat_axis=0, til...  12 us
    all_to_all x1, starting transfers between devices, on_device(): lax.all_to_all(grad_long, 'ctx', split_axis=0, concat_axis=1, tiled=True)  9.67 us
  transfers between devices with their start and end apart: 12, of which 7 were waited for; matrix products, arithmetic and copies ran while one was open for 8% of the time, Pallas kernels for 0%

profile of v1, /device:TPU:1, one launch (start us, length us, event | category | flops | bytes accessed | tf_op | source)
XLA Modules:
  0.0 471.6 jit_solution(10600531233884873021)
XLA Ops:
  0.6 0.8 slice.242
  1.5 4.6 collective-permute-start
  10.4 15.5 %all-to-all-start = ((bf16[64,2,256]{2,1,0:T(2,128)(2,1)}), bf16[64,2,256]{2,1,0:T(2,128)(2,1)S(1)}, u32[]{:S(2)}, u32[]{:S(2)}) async-start(bf16[64,2,256]{2,1,0:T(2,128)(2,1)} %all_to_all.60), calls=%async_computation | async-start | bytes 131072 | tf_op jit(solution)/shard_map/all_to_all | solution.py:199
  26.0 3.5 collective-permute-start.2
  29.6 2.2 collective-permute-start.1
  35.7 2.4 all-to-all-done
  38.1 9.7 %all-to-all-start.3 = ((bf16[64,2,256]{2,1,0:T(2,128)(2,1)}), bf16[64,2,256]{2,1,0:T(2,128)(2,1)S(1)}, u32[]{:S(2)}, u32[]{:S(2)}) async-start(bf16[64,2,256]{2,1,0:T(2,128)(2,1)} %all_to_all.67), calls=%async_computation.3 | async-start | bytes 131072 | tf_op jit(solution)/shard_map/all_to_all | solution.py:205
  51.7 7.9 %all-to-all-done.3 = bf16[64,2,256]{2,1,0:T(2,128)(2,1)S(1)} async-done(((bf16[64,2,256]{2,1,0:T(2,128)(2,1)}), bf16[64,2,256]{2,1,0:T(2,128)(2,1)S(1)}, u32[]{:S(2)}, u32[]{:S(2)}) %all-to-all-start.3) | async-done | bytes 65568 | tf_op jit(solution)/shard_map/all_to_all | solution.py:205
  60.4 0.8 convolution_bitcast_fusion.1
  67.6 11.5 %fusion.19 = f32[2,128,128]{2,1,0:T(8,128)S(1)} fusion(f32[2,256,128]{1,2,0:T(8,128)S(1)} %convolution_subtract_fusion.1, f32[2,256,128]{1,2,0:T(8,128)S(1)} %convolution_add_fusion.1, f32[256,128]{0,1:T(8,128)S(1)} %copy.206, f32[256,128]{0,1:T(8,128)S(1)} %copy.204), kind=kOutput, calls=%fused_computation.45 | convolution fusion | flops 101318656 | bytes 917504 | tf_op jit(solution)/shard_map/kt,nks->nts/dot_general | solution.py:95
  79.1 0.9 fusion.2
  80.9 4.8 %all-to-all-start.4 = ((bf16[2,64,256]{2,0,1:T(2,128)(2,1)}), bf16[2,64,256]{2,0,1:T(2,128)(2,1)S(1)}, u32[]{:S(2)}, u32[]{:S(2)}) async-start(bf16[2,64,256]{2,0,1:T(2,128)(2,1)} %copy.236), calls=%async_computation.4 | async-start | bytes 131072 | tf_op jit(solution)/shard_map/all_to_all | solution.py:210
  86.0 12.0 %all-to-all-done.4 = bf16[2,64,256]{2,0,1:T(2,128)(2,1)S(1)} async-done(((bf16[2,64,256]{2,0,1:T(2,128)(2,1)}), bf16[2,64,256]{2,0,1:T(2,128)(2,1)S(1)}, u32[]{:S(2)}, u32[]{:S(2)}) %all-to-all-start.4) | async-done | bytes 65568 | tf_op jit(solution)/shard_map/all_to_all | solution.py:210
  98.5 2.3 collective-permute-start.5
  101.9 6.0 %all-to-all-start.1 = ((bf16[64,2,256]{2,1,0:T(2,128)(2,1)}), bf16[64,2,256]{2,1,0:T(2,128)(2,1)S(1)}, u32[]{:S(2)}, u32[]{:S(2)}) async-start(bf16[64,2,256]{2,1,0:T(2,128)(2,1)} %all_to_all.63), calls=%async_computation.1 | async-start | bytes 131072 | tf_op jit(solution)/shard_map/all_to_all | solution.py:198
  108.0 2.4 collective-permute-start.4
  110.4 1.0 fusion.37
  111.4 2.1 collective-permute-done.4
  113.5 1.0 fusion.44
  114.5 5.6 %all-to-all-done.1 = bf16[64,2,256]{2,1,0:T(2,128)(2,1)S(1)} async-done(((bf16[64,2,256]{2,1,0:T(2,128)(2,1)}), bf16[64,2,256]{2,1,0:T(2,128)(2,1)S(1)}, u32[]{:S(2)}, u32[]{:S(2)}) %all-to-all-start.1) | async-done | bytes 65568 | tf_op jit(solution)/shard_map/all_to_all | solution.py:198
  124.0 0.8 multiply_add_fusion
  127.4 0.9 fusion.12
  128.3 0.9 fusion.8
  130.0 7.0 %all-to-all-start.5 = ((bf16[2,64,256]{2,0,1:T(2,128)(2,1)}), bf16[2,64,256]{2,0,1:T(2,128)(2,1)S(1)}, u32[]{:S(2)}, u32[]{:S(2)}) async-start(bf16[2,64,256]{2,0,1:T(2,128)(2,1)} %copy.242), calls=%async_computation.5 | async-start | bytes 131072 | tf_op jit(solution)/shard_map/all_to_all | solution.py:211
  139.6 0.9 fusion.26
  140.5 0.9 fusion.4
  142.3 6.9 %all-to-all-done.5 = bf16[2,64,256]{2,0,1:T(2,128)(2,1)S(1)} async-done(((bf16[2,64,256]{2,0,1:T(2,128)(2,1)}), bf16[2,64,256]{2,0,1:T(2,128)(2,1)S(1)}, u32[]{:S(2)}, u32[]{:S(2)}) %all-to-all-start.5) | async-done | bytes 65568 | tf_op jit(solution)/shard_map/all_to_all | solution.py:211
  149.2 5.8 %all-to-all-start.2 = ((bf16[2,64,256]{2,0,1:T(2,128)(2,1)}), bf16[2,64,256]{2,0,1:T(2,128)(2,1)S(1)}, u32[]{:S(2)}, u32[]{:S(2)}) async-start(bf16[2,64,256]{2,0,1:T(2,128)(2,1)} %copy.223), calls=%async_computation.2 | async-start | bytes 131072 | tf_op jit(solution)/shard_map/all_to_all | solution.py:204
  156.2 27.7 %psum.22 = f32[64,33]{0,1:T(8,128)S(1)} all-reduce(f32[64,33]{0,1:T(8,128)S(1)} %fusion.423), channel_id=1, replica_groups=mesh['ctx'=64,'tp'=8] {'tp'}, use_global_device_ids=true, to_apply=%region_1.2 | all-reduce | flops 2112 | bytes 16896 | tf_op jit(solution)/shard_map/psum | solution.py:229
  183.9 275.7 %all-reduce = (f32[128,64]{0,1:T(8,128)S(1)}, f32[64,33]{0,1:T(8,128)S(1)}) all-reduce(f32[128,64]{0,1:T(8,128)S(1)} %fusion.417, f32[64,33]{0,1:T(8,128)S(1)} %psum.22), channel_id=1, replica_groups=mesh['ctx'=64,'tp'=8] {'ctx'}, use_global_device_ids=true, to_apply=%region_0.1 | all-reduce | flops 10304 | bytes 82432 | tf_op jit(solution)/shard_map/psum | solution.py:228
  461.0 8.4 %collective-permute-start.3 = (bf16[128,6]{1,0:T(8,128)(2,1)S(1)}, bf16[128,6]{1,0:T(8,128)(2,1)S(1)}, u32[]{:S(2)}, u32[]{:S(2)}) collective-permute-start(bf16[128,6]{1,0:T(8,128)(2,1)S(1)} %slice.333), channel_id=1, source_target_pairs={{8,0},{16,8},{24,16},{32,24},{40,32},{48,40},{56,48},{64,56},{72,6... | collective-permute-start | bytes 4616 | tf_op jit(solution)/shard_map/ppermute | solution.py:13
  470.4 1.0 fusion.51
  (132 shorter events, 36.1 us)
Async XLA Ops:
  0.6 8.8 %copy-start = (f32[128,64]{0,1:T(8,128)S(1)}, f32[128,64]{0,1:T(8,128)}, u32[]{:S(2)}) copy-start(f32[128,64]{0,1:T(8,128)} %param.16) | copy-start | bytes 98308
  1.5 32.3 %collective-permute-start = (bf16[128,6]{1,0:T(8,128)(2,1)S(1)}, bf16[128,6]{1,0:T(8,128)(2,1)S(1)}, u32[]{:S(2)}, u32[]{:S(2)}) collective-permute-start(bf16[128,6]{1,0:T(8,128)(2,1)S(1)} %slice.242), channel_id=1, source_target_pairs={{0,8},{8,16},{16,24},{24,32},{32,40},{40,48},{48,56},{56,64},{64,7... | collective-permute-start | bytes 4616 | tf_op jit(solution)/shard_map/ppermute | solution.py:13
  7.5 0.7 copy-start.9
  8.2 0.7 copy-start.5
  8.2 0.7 copy-start.7
  10.4 15.5 %copy-start.3 = (bf16[128,256]{1,0:T(8,128)(2,1)S(1)}, bf16[128,256]{1,0:T(8,128)(2,1)}, u32[]{:S(2)}) copy-start(bf16[128,256]{1,0:T(8,128)(2,1)} %param.12) | copy-start | bytes 196612
  10.4 27.7 %all-to-all-start = ((bf16[64,2,256]{2,1,0:T(2,128)(2,1)}), bf16[64,2,256]{2,1,0:T(2,128)(2,1)S(1)}, u32[]{:S(2)}, u32[]{:S(2)}) async-start(bf16[64,2,256]{2,1,0:T(2,128)(2,1)} %all_to_all.60), calls=%async_computation | async-start | bytes 131072 | tf_op jit(solution)/shard_map/all_to_all | solution.py:199
  25.9 3.6 copy-start.4
  26.0 59.8 %collective-permute-start.2 = (bf16[128,6]{1,0:T(8,128)(2,1)S(1)}, bf16[128,6]{1,0:T(8,128)(2,1)S(1)}, u32[]{:S(2)}, u32[]{:S(2)}) collective-permute-start(bf16[128,6]{1,0:T(8,128)(2,1)S(1)} %slice.274), channel_id=1, source_target_pairs={{0,8},{8,16},{16,24},{24,32},{32,40},{40,48},{48,56},{56,64},{64,7... | collective-permute-start | bytes 4616 | tf_op jit(solution)/shard_map/ppermute | solution.py:13
  29.6 2.7 copy-start.6
  29.6 56.3 %collective-permute-start.1 = (bf16[128,6]{1,0:T(8,128)(2,1)S(1)}, bf16[128,6]{1,0:T(8,128)(2,1)S(1)}, u32[]{:S(2)}, u32[]{:S(2)}) collective-permute-start(bf16[128,6]{1,0:T(8,128)(2,1)S(1)} %slice.258), channel_id=1, source_target_pairs={{0,8},{8,16},{16,24},{24,32},{32,40},{40,48},{48,56},{56,64},{64,7... | collective-permute-start | bytes 4616 | tf_op jit(solution)/shard_map/ppermute | solution.py:13
  33.0 0.9 copy-start.2
  33.1 0.7 copy-start.8
  33.8 0.8 copy-start.1
  38.1 21.5 %all-to-all-start.3 = ((bf16[64,2,256]{2,1,0:T(2,128)(2,1)}), bf16[64,2,256]{2,1,0:T(2,128)(2,1)S(1)}, u32[]{:S(2)}, u32[]{:S(2)}) async-start(bf16[64,2,256]{2,1,0:T(2,128)(2,1)} %all_to_all.67), calls=%async_computation.3 | async-start | bytes 131072 | tf_op jit(solution)/shard_map/all_to_all | solution.py:205
  80.9 17.0 %all-to-all-start.4 = ((bf16[2,64,256]{2,0,1:T(2,128)(2,1)}), bf16[2,64,256]{2,0,1:T(2,128)(2,1)S(1)}, u32[]{:S(2)}, u32[]{:S(2)}) async-start(bf16[2,64,256]{2,0,1:T(2,128)(2,1)} %copy.236), calls=%async_computation.4 | async-start | bytes 131072 | tf_op jit(solution)/shard_map/all_to_all | solution.py:210
  98.5 11.8 %collective-permute-start.5 = (bf16[128,6]{1,0:T(8,128)(2,1)S(1)}, bf16[128,6]{1,0:T(8,128)(2,1)S(1)}, u32[]{:S(2)}, u32[]{:S(2)}) collective-permute-start(bf16[128,6]{1,0:T(8,128)(2,1)S(1)} %slice.349), channel_id=1, source_target_pairs={{8,0},{16,8},{24,16},{32,24},{40,32},{48,40},{56,48},{64,56},{72,6... | collective-permute-start | bytes 4616 | tf_op jit(solution)/shard_map/ppermute | solution.py:13
  101.9 18.2 %all-to-all-start.1 = ((bf16[64,2,256]{2,1,0:T(2,128)(2,1)}), bf16[64,2,256]{2,1,0:T(2,128)(2,1)S(1)}, u32[]{:S(2)}, u32[]{:S(2)}) async-start(bf16[64,2,256]{2,1,0:T(2,128)(2,1)} %all_to_all.63), calls=%async_computation.1 | async-start | bytes 131072 | tf_op jit(solution)/shard_map/all_to_all | solution.py:198
  108.0 5.5 %collective-permute-start.4 = (bf16[128,6]{1,0:T(8,128)(2,1)S(1)}, bf16[128,6]{1,0:T(8,128)(2,1)S(1)}, u32[]{:S(2)}, u32[]{:S(2)}) collective-permute-start(bf16[128,6]{1,0:T(8,128)(2,1)S(1)} %slice.341), channel_id=1, source_target_pairs={{8,0},{16,8},{24,16},{32,24},{40,32},{48,40},{56,48},{64,56},{72,6... | collective-permute-start | bytes 4616 | tf_op jit(solution)/shard_map/ppermute | solution.py:13
  130.0 19.1 %all-to-all-start.5 = ((bf16[2,64,256]{2,0,1:T(2,128)(2,1)}), bf16[2,64,256]{2,0,1:T(2,128)(2,1)S(1)}, u32[]{:S(2)}, u32[]{:S(2)}) async-start(bf16[2,64,256]{2,0,1:T(2,128)(2,1)} %copy.242), calls=%async_computation.5 | async-start | bytes 131072 | tf_op jit(solution)/shard_map/all_to_all | solution.py:211
  149.2 311.1 %all-to-all-start.2 = ((bf16[2,64,256]{2,0,1:T(2,128)(2,1)}), bf16[2,64,256]{2,0,1:T(2,128)(2,1)S(1)}, u32[]{:S(2)}, u32[]{:S(2)}) async-start(bf16[2,64,256]{2,0,1:T(2,128)(2,1)} %copy.223), calls=%async_computation.2 | async-start | bytes 131072 | tf_op jit(solution)/shard_map/all_to_all | solution.py:204
  461.0 9.3 %collective-permute-start.3 = (bf16[128,6]{1,0:T(8,128)(2,1)S(1)}, bf16[128,6]{1,0:T(8,128)(2,1)S(1)}, u32[]{:S(2)}, u32[]{:S(2)}) collective-permute-start(bf16[128,6]{1,0:T(8,128)(2,1)S(1)} %slice.333), channel_id=1, source_target_pairs={{8,0},{16,8},{24,16},{32,24},{40,32},{48,40},{56,48},{64,56},{72,6... | collective-permute-start | bytes 4616 | tf_op jit(solution)/shard_map/ppermute | solution.py:13
